TPU v7x, 32 devices: a whole 2x2x4 slice. The times are simulated.
32 devices in a mesh: band: 16 (over z, y, x), lev: 2 (over core).
Axes of the slice: x: 2, y: 2, z: 4, core: 2. Of those that a mesh axis runs over, the one named last changes fastest.
Arguments:
- arrival_adjoint: bfloat16 [160, 64, 1536], P('band', 'lev'), may hold values from -6 to 6
- interp_tiles: bfloat16 [160, 12, 128, 128], P('band'), may hold values from -0.5 to 0.5
- departure_block: int32 [160, 12], P('band'), may hold values from 0 to 239
- slot_wavenumber: int32 [768], replicated, may hold values from 0 to 767, each once
- legendre: bfloat16 [768, 160, 768], P('band', None, 'lev'), may hold values from -0.5 to 0.5
Outputs:
- spectral: bfloat16 [768, 64, 2, 768], P('band', None, None, 'lev')
Inputs may be any that keep to these rules, and one draw needn't show every extreme that they name: `departure_block`: an entry d of the tile at latitude l names latitude L + d // 12 - 5 and longitude block d % 12, where L is the first latitude of l's band of 10. `slot_wavenumber`: each wavenumber below 768 stands in exactly one slot.
All inputs are finite; a program needn't handle non-finite values.
Results may differ from a plain program's by a relative error of at most 0.015.
Values may be sent and summed in bfloat16 or wider, within the bound.
No kernel may reach another device: no remote copies, remote signals or barrier semaphores. Data moves between devices by JAX's collectives and lax.ppermute only.
A program may use at most 128 MiB of HBM per device.

v0:
```python
import math
import jax
import jax.numpy as jnp
from jax import lax
from jax.sharding import PartitionSpec as P


def passed_along(block, axis, distance):
    devices = range(lax.axis_size(axis))
    route = [(i - distance, i) for i in devices if i - distance in devices]
    return lax.ppermute(block, axis, route)


def wave_table(slot_wavenumber, lon_count):
    column = lax.iota(jnp.int32, lon_count)[:, None]
    product = column * slot_wavenumber[None, :] % lon_count
    angle = product.astype(jnp.float32) * (2.0 * math.pi / lon_count)
    factor = math.sqrt(2.0 / lon_count)
    return jnp.stack([jnp.cos(angle) * factor, jnp.sin(angle) * factor]).astype(jnp.bfloat16)


def local(arrival_adjoint, interp_tiles, departure_block, slot_wavenumber, legendre):
    lat_count, level_count, lon_count = arrival_adjoint.shape
    block_count = interp_tiles.shape[1]
    tile_width = interp_tiles.shape[2]
    rim_rows = lat_count // 2
    tiles = arrival_adjoint.reshape(lat_count, level_count, block_count, tile_width)
    contrib = jnp.einsum("lvbi,lbik->lbvk", tiles, interp_tiles, preferred_element_type=jnp.float32)
    contrib = contrib.reshape(lat_count * block_count, level_count * tile_width)
    upper = contrib.astype(jnp.bfloat16)
    lower = (contrib - upper.astype(jnp.float32)).astype(jnp.bfloat16)
    extended = (lat_count + 2 * rim_rows) * block_count
    targets = (lax.iota(jnp.int32, extended)[:, None] == departure_block.reshape(1, -1)).astype(
        jnp.bfloat16
    )
    placed = jnp.dot(targets, upper, preferred_element_type=jnp.float32) + jnp.dot(
        targets, lower, preferred_element_type=jnp.float32
    )
    placed = placed.reshape(lat_count + 2 * rim_rows, block_count, level_count, tile_width)
    from_below = passed_along(
        placed[lat_count + rim_rows :].astype(jnp.bfloat16), "band", 1
    ).astype(jnp.float32)
    from_above = passed_along(placed[:rim_rows].astype(jnp.bfloat16), "band", -1).astype(
        jnp.float32
    )
    grid = placed[rim_rows : rim_rows + lat_count] + jnp.concatenate(
        [from_below, from_above], axis=0
    )
    grid = grid.astype(jnp.bfloat16)
    table = wave_table(slot_wavenumber, lon_count).reshape(2, block_count, tile_width, -1)
    fourier = jnp.einsum("lbvt,cbts->scvl", grid, table, preferred_element_type=jnp.float32).astype(
        jnp.bfloat16
    )
    wave_count = fourier.shape[0]
    flat = fourier.reshape(wave_count, -1)
    shared = lax.all_gather(flat[None], "lev", axis=0, tiled=True)
    owned = lax.all_to_all(shared, "band", split_axis=1, concat_axis=2, tiled=True)
    group_count = owned.shape[0]
    slot_count = owned.shape[1]
    band_count = lax.axis_size("band")
    degree_count = legendre.shape[2]
    owned = owned.reshape(group_count, slot_count, band_count, 2, level_count, lat_count)
    tables = legendre.reshape(slot_count, band_count, lat_count, degree_count)
    spectral = jnp.einsum("gsbcvl,sbln->sgvcn", owned, tables, preferred_element_type=jnp.float32)
    spectral = spectral.reshape(slot_count, group_count * level_count, 2, degree_count)
    degree = lax.axis_index("lev") * degree_count + lax.iota(jnp.int32, degree_count)
    owned_waves = lax.dynamic_slice_in_dim(
        slot_wavenumber, lax.axis_index("band") * slot_count, slot_count
    )
    keep = degree[None, :] >= owned_waves[:, None]
    return jnp.where(keep[:, None, None, :], spectral, 0.0).astype(jnp.bfloat16)


def solution(mesh):
    placed = (
        P("band", "lev", None),
        P("band", None, None, None),
        P("band", None),
        P(),
        P("band", None, "lev"),
    )
    return jax.shard_map(
        local, mesh=mesh, in_specs=placed, out_specs=P("band", None, None, "lev"), check_vma=False
    )
```

profile of v0, /device:TPU:12, one launch (start us, length us, event | category | flops | bytes accessed | tf_op | source)
XLA Modules:
  0.0 174.6 jit_solution(13239174042174371197)
XLA Ops:
  6.5 0.0 copy-start
  6.5 0.0 all-gather.2.cloned.1.call-start
  6.5 0.9 eq.18
  7.4 0.4 copy-done
  7.8 3.2 %fusion.20 = f32[10,12,32,128]{3,2,1,0:T(8,128)S(1)} fusion(bf16[10,12,128,128]{3,2,1,0:T(8,128)(2,1)} %param.6, bf16[10,32,1536]{2,1,0:T(8,128)(2,1)S(1)} %copy-done), kind=kOutput, calls=%fused_computation.28 | convolution fusion | flops 125829120 | bytes 6881280 | tf_op jit(solution)/shard_map/lvbi,lbik->lbvk/dot_general | solution.py:28
  11.0 1.5 fusion.15
  12.5 1.6 fusion.30
  14.2 0.1 fusion.29
  14.3 0.1 copy.44
  14.4 3.4 %collective-permute-start = (bf16[5,12,32,128]{3,2,1,0:T(8,128)(2,1)S(1)}, bf16[5,12,32,128]{3,2,1,0:T(8,128)(2,1)S(1)}, u32[]{:S(2)}, u32[]{:S(2)}) collective-permute-start(bf16[5,12,32,128]{3,2,1,0:T(8,128)(2,1)S(1)} %bitcast.81), channel_id=1, source_target_pairs={{0,2},{2,4},{4,6},{6,8},{8,10},{10,12},{12,14},{14,16},{16,18},{18... | collective-permute-start | bytes 1474568 | tf_op jit(solution)/shard_map/ppermute | solution.py:11
  17.8 0.1 copy.45
  18.0 3.3 %collective-permute-start.1 = (bf16[5,12,32,128]{3,2,1,0:T(8,128)(2,1)S(1)}, bf16[5,12,32,128]{3,2,1,0:T(8,128)(2,1)S(1)}, u32[]{:S(2)}, u32[]{:S(2)}) collective-permute-start(bf16[5,12,32,128]{3,2,1,0:T(8,128)(2,1)S(1)} %bitcast.82), channel_id=1, source_target_pairs={{2,0},{4,2},{6,4},{8,6},{10,8},{12,10},{14,12},{16,14},{18,16},{20... | collective-permute-start | bytes 1474568 | tf_op jit(solution)/shard_map/ppermute | solution.py:11
  21.3 0.0 copy-start.2
  21.4 0.1 slice_bitcast_fusion
  21.5 0.3 copy.43
  21.9 0.2 copy-done.2
  22.0 20.6 %multiply_convert_fusion.1 = (bf16[1,12,128,768]{3,2,1,0:T(8,128)(2,1)S(1)}, bf16[1,12,128,768]{3,2,1,0:T(8,128)(2,1)S(1)}) fusion(s32[768]{0:T(1024)S(1)} %copy-done.2, s32[12,128]{1,0:T(8,128)S(1)} %multiply_add_fusion), kind=kLoop, calls=%fused_computation.13 | loop fusion | flops 15335424 | bytes 4727808 | tf_op jit(solution)/shard_map/convert.3
  42.6 0.0 collective-permute-done
  42.6 0.0 collective-permute-done.1
  42.6 1.7 fusion.16
  44.3 0.6 copy.25
  44.9 0.4 broadcast_in_dim_reshape.3
  45.3 1.3 copy.26
  46.6 0.0 all-gather.2.cloned.1.call-update
  46.7 11.0 %all-gather.2.cloned.1.call-done = bf16[2,768,640]{2,1,0:T(8,128)(2,1)} async-done(((bf16[1,768,640]{2,1,0:T(8,128)(2,1)}), bf16[2,768,640]{2,1,0:T(8,128)(2,1)}) %all-gather.2.cloned.1.call-update) | async-done | bytes 1966096 | tf_op jit(solution)/shard_map/all_gather | solution.py:56
  57.7 4.8 %copy.27 = bf16[2,768,640]{2,0,1:T(2,128)(2,1)} copy(bf16[2,768,640]{2,1,0:T(8,128)(2,1)} %all-gather.2.cloned.1.call-done) | data formatting | bytes 3932160 | tf_op jit(solution)/shard_map/all_gather | solution.py:56
  62.6 7.0 %all-to-all-start = ((bf16[2,768,640]{2,0,1:T(2,128)(2,1)}), bf16[2,768,640]{2,0,1:T(2,128)(2,1)S(1)}, u32[]{:S(2)}, u32[]{:S(2)}) async-start(bf16[2,768,640]{2,0,1:T(2,128)(2,1)} %copy.27), calls=%async_computation | async-start | bytes 3932160 | tf_op jit(solution)/shard_map/all_to_all | solution.py:57
  69.5 7.4 %copy.30 = bf16[48,160,384]{2,0,1:T(8,128)(2,1)} copy(bf16[48,160,384]{2,1,0:T(8,128)(2,1)} %param.9) | data formatting | bytes 11796480 | tf_op args[4]
  77.0 0.1 dynamic_slice.3
  77.0 0.1 broadcast_compare_fusion
  77.1 38.1 %all-to-all-done = bf16[2,768,640]{2,0,1:T(2,128)(2,1)S(1)} async-done(((bf16[2,768,640]{2,0,1:T(2,128)(2,1)}), bf16[2,768,640]{2,0,1:T(2,128)(2,1)S(1)}, u32[]{:S(2)}, u32[]{:S(2)}) %all-to-all-start) | async-done | bytes 1966112 | tf_op jit(solution)/shard_map/all_to_all | solution.py:57
  115.3 1.5 copy.28
  116.8 6.7 %copy.29 = bf16[2,48,16,640]{1,2,3,0:T(8,128)(2,1)} copy(bf16[2,48,16,640]{3,1,2,0:T(8,128)(2,1)} %bitcast.75) | data formatting | bytes 3932160 | tf_op jit(solution)/shard_map/all_to_all | solution.py:57
  123.5 15.3 %copy.31 = bf16[2,48,16,2,32,10]{4,2,5,3,0,1:T(8,128)(2,1)} copy(bf16[2,48,16,2,32,10]{1,2,5,4,3,0:T(8,128)(2,1)} %bitcast.72) | data formatting | bytes 3932160 | tf_op jit(solution)/shard_map/reshape | solution.py:62
  138.9 12.0 %fusion.11 = bf16[48,2,32,2,384]{4,2,3,1,0:T(8,128)(2,1)} fusion(bf16[2,48,16,2,32,10]{4,2,5,3,0,1:T(8,128)(2,1)} %copy.31, bf16[48,16,10,384,1,1]{3,0,2,1,5,4:T(8,128)(2,1)} %bitcast.71), kind=kOutput, calls=%fused_computation.18 | convolution fusion | flops 754974720 | bytes 12582912 | tf_op jit(solution)/shard_map/gsbcvl,sbln->sgvcn/dot_general | solution.py:64
  150.9 3.2 %copy.33 = bf16[48,2,32,2,384]{4,2,1,3,0:T(8,128)(2,1)S(1)} copy(bf16[48,2,32,2,384]{4,2,3,1,0:T(8,128)(2,1)} %fusion.11) | data formatting | bytes 9437184 | tf_op jit(solution)/shard_map/gsbcvl,sbln->sgvcn/transpose | solution.py:64
  154.1 0.0 copy-start.1
  154.1 4.2 %fusion = bf16[48,64,2,384]{3,1,2,0:T(8,128)(2,1)} fusion(bf16[48,2,32,2,384]{4,2,1,3,0:T(8,128)(2,1)S(1)} %copy.33, pred[48,384]{1,0:T(8,128)(4,1)S(1)} %broadcast_compare_fusion), kind=kLoop, calls=%fused_computation.1 | loop fusion | flops 2359296 | bytes 9455616 | tf_op jit(solution)/shard_map/convert_element_type | solution.py:71
  158.4 9.4 %copy.34 = bf16[48,64,2,384]{3,2,1,0:T(2,128)(2,1)} copy(bf16[48,64,2,384]{3,1,2,0:T(8,128)(2,1)} %fusion) | data formatting | bytes 9437184 | tf_op jit(solution)/shard_map/convert_element_type | solution.py:71
  167.7 0.0 copy-done.1
  (4 shorter events, 0.1 us)
Async XLA Ops:
  6.5 1.2 copy-start
  6.5 51.2 %all-gather.2.cloned.1.call-start = ((), (), s32[]{:S(2)}) async-start(), calls=%async_computation.1 | async-start | bytes 2949120 | tf_op jit(solution)/shard_map/all_gather | solution.py:56
  14.4 28.2 %collective-permute-start = (bf16[5,12,32,128]{3,2,1,0:T(8,128)(2,1)S(1)}, bf16[5,12,32,128]{3,2,1,0:T(8,128)(2,1)S(1)}, u32[]{:S(2)}, u32[]{:S(2)}) collective-permute-start(bf16[5,12,32,128]{3,2,1,0:T(8,128)(2,1)S(1)} %bitcast.81), channel_id=1, source_target_pairs={{0,2},{2,4},{4,6},{6,8},{8,10},{10,12},{12,14},{14,16},{16,18},{18... | collective-permute-start | bytes 1474568 | tf_op jit(solution)/shard_map/ppermute | solution.py:11
  18.0 24.7 %collective-permute-start.1 = (bf16[5,12,32,128]{3,2,1,0:T(8,128)(2,1)S(1)}, bf16[5,12,32,128]{3,2,1,0:T(8,128)(2,1)S(1)}, u32[]{:S(2)}, u32[]{:S(2)}) collective-permute-start(bf16[5,12,32,128]{3,2,1,0:T(8,128)(2,1)S(1)} %bitcast.82), channel_id=1, source_target_pairs={{2,0},{4,2},{6,4},{8,6},{10,8},{12,10},{14,12},{16,14},{18,16},{20... | collective-permute-start | bytes 1474568 | tf_op jit(solution)/shard_map/ppermute | solution.py:11
  21.3 0.7 copy-start.2
  62.6 52.7 %all-to-all-start = ((bf16[2,768,640]{2,0,1:T(2,128)(2,1)}), bf16[2,768,640]{2,0,1:T(2,128)(2,1)S(1)}, u32[]{:S(2)}, u32[]{:S(2)}) async-start(bf16[2,768,640]{2,0,1:T(2,128)(2,1)} %copy.27), calls=%async_computation | async-start | bytes 3932160 | tf_op jit(solution)/shard_map/all_to_all | solution.py:57
  154.1 13.6 %copy-start.1 = (bf16[10,32,1536]{2,1,0:T(8,128)(2,1)S(1)}, bf16[10,32,1536]{2,1,0:T(8,128)(2,1)}, u32[]{:S(2)}) copy-start(bf16[10,32,1536]{2,1,0:T(8,128)(2,1)} %param.5) | copy-start | bytes 2949124
Sparse Core Ops, SparseCore 0:
  46.8 10.8 all-gather.1
where the time goes:
time: 175 us
  local copies, waits for them, and re-layouts  53.1 us (30%)
  waiting for transfers between devices  49.2 us (28%)
  other arithmetic  24.9 us (14%)
  matrix products  20.1 us (11%)
  starting transfers between devices  13.7 us (8%)
  between operations  13.6 us (8%)
    all_to_all x1, waiting for transfers between devices, local(): lax.all_to_all(shared, 'band', split_axis=1, concat_axis=2, tiled=True)  38.1 us
    another operation x1, other arithmetic  20.6 us
    reshape x1, local copies, waits for them, and re-layouts, local(): owned.reshape(group_count, slot_count, band_count, 2, level_count, lat_co...  15.3 us
    dot_general x1, matrix products, local(): jnp.einsum('gsbcvl,sbln->sgvcn', owned, tables, preferred_element_type=jn...  12 us
    all_gather x1, waiting for transfers between devices, local(): shared = lax.all_gather(flat[None], 'lev', axis=0, tiled=True)  11 us
    convert_element_type x1, local copies, waits for them, and re-layouts, local(): return jnp.where(keep[:, None, None, :], spectral, 0.0).astype(jnp.bfloat16)  9.37 us
    unnamed x13, local copies, waits for them, and re-layouts  8.71 us
    all_to_all x2, local copies, waits for them, and re-layouts, local(): lax.all_to_all(shared, 'band', split_axis=1, concat_axis=2, tiled=True)  8.26 us
  transfers between devices with their start and end apart: 4, of which 2 were waited for; matrix products, arithmetic and copies ran while one was open for 16% of the time, Pallas kernels for 0%

commit v1 on v0

--- a/solution.py
+++ b/solution.py
@@ -54,7 +54,10 @@
     wave_count = fourier.shape[0]
     flat = fourier.reshape(wave_count, -1)
     shared = lax.all_gather(flat[None], "lev", axis=0, tiled=True)
-    owned = lax.all_to_all(shared, "band", split_axis=1, concat_axis=2, tiled=True)
+    owned = jnp.concatenate(
+        lax.all_to_all(jnp.stack(jnp.split(shared, lax.axis_size("band"), axis=1)), "band", 0, 0),
+        axis=2,
+    )
     group_count = owned.shape[0]
     slot_count = owned.shape[1]
     band_count = lax.axis_size("band")

time: 175 us -> 193 us (1.10)
  local copies, waits for them, and re-layouts: 53.1 us -> 70.4 us
    unnamed x13 -> x28, local copies, waits for them, and re-layouts: 8.71 us -> 32.3 us
    another operation x0 -> x2, local copies, waits for them, and re-layouts: none -> 16.9 us  [the longest x1 15.3 us: local(): owned.reshape(group_count, slot_count, band_count, 2, level_count, lat_co...]
    reshape x1 -> x0, local copies, waits for them, and re-layouts: 15.3 us -> none  [local(): owned.reshape(group_count, slot_count, band_count, 2, level_count, lat_co...]
    all_gather x1 -> x0, local copies, waits for them, and re-layouts: 4.84 us -> none  [local(): shared = lax.all_gather(flat[None], 'lev', axis=0, tiled=True)]
    all_to_all x2 -> x1, local copies, waits for them, and re-layouts: 8.26 us -> 5.27 us  [local(): lax.all_to_all(jnp.stack(jnp.split(shared, lax.axis_size('band'), axis=1)...]
  transfers between devices with their start and end apart: 4 -> 4, of which waited for: 2 -> 2; matrix products, arithmetic and copies ran while one was open for 16% -> 15% of each run, Pallas kernels for 0% -> 0%
where the time goes in v1:
time: 193 us; the launch traced here: 192 us
  local copies, waits for them, and re-layouts  70.4 us (36%)
  waiting for transfers between devices  49.2 us (25%)
  other arithmetic  24.9 us (13%)
  matrix products  20.1 us (10%)
  starting transfers between devices  13.7 us (7%)
  between operations  13.6 us (7%)
    all_to_all x1, waiting for transfers between devices, local(): lax.all_to_all(jnp.stack(jnp.split(shared, lax.axis_size('band'), axis=1)...  38.1 us
    unnamed x28, local copies, waits for them, and re-layouts  32.3 us
    another operation x1, other arithmetic  20.6 us
    another operation x1, local copies, waits for them, and re-layouts, local(): owned.reshape(group_count, slot_count, band_count, 2, level_count, lat_co...  15.3 us
    dot_general x1, matrix products, local(): jnp.einsum('gsbcvl,sbln->sgvcn', owned, tables, preferred_element_type=jn...  12 us
    all_gather x1, waiting for transfers between devices, local(): shared = lax.all_gather(flat[None], 'lev', axis=0, tiled=True)  11 us
    convert_element_type x1, local copies, waits for them, and re-layouts, local(): return jnp.where(keep[:, None, None, :], spectral, 0.0).astype(jnp.bfloat16)  9.46 us
    all_to_all x1, starting transfers between devices, local(): lax.all_to_all(jnp.stack(jnp.split(shared, lax.axis_size('band'), axis=1)...  6.96 us
  transfers between devices with their start and end apart: 4, of which 2 were waited for; matrix products, arithmetic and copies ran while one was open for 15% of the time, Pallas kernels for 0%

profile of v1, /device:TPU:12, one launch (start us, length us, event | category | flops | bytes accessed | tf_op | source)
XLA Modules:
  0.0 192.0 jit_solution(2978415815893470104)
XLA Ops:
  6.5 0.9 eq.18
  7.4 0.4 copy-done
  7.8 3.2 %fusion.20 = f32[10,12,32,128]{3,2,1,0:T(8,128)S(1)} fusion(bf16[10,12,128,128]{3,2,1,0:T(8,128)(2,1)} %param.6, bf16[10,32,1536]{2,1,0:T(8,128)(2,1)S(1)} %copy-done), kind=kOutput, calls=%fused_computation.28 | convolution fusion | flops 125829120 | bytes 6881280 | tf_op jit(solution)/shard_map/lvbi,lbik->lbvk/dot_general | solution.py:28
  11.0 1.5 fusion.15
  12.5 1.6 fusion.46
  14.2 0.1 fusion.45
  14.3 0.1 copy.34
  14.4 3.4 %collective-permute-start = (bf16[5,12,32,128]{3,2,1,0:T(8,128)(2,1)S(1)}, bf16[5,12,32,128]{3,2,1,0:T(8,128)(2,1)S(1)}, u32[]{:S(2)}, u32[]{:S(2)}) collective-permute-start(bf16[5,12,32,128]{3,2,1,0:T(8,128)(2,1)S(1)} %bitcast.143), channel_id=1, source_target_pairs={{0,2},{2,4},{4,6},{6,8},{8,10},{10,12},{12,14},{14,16},{16,18},{18... | collective-permute-start | bytes 1474568 | tf_op jit(solution)/shard_map/ppermute | solution.py:11
  17.8 0.1 copy.35
  18.0 3.3 %collective-permute-start.1 = (bf16[5,12,32,128]{3,2,1,0:T(8,128)(2,1)S(1)}, bf16[5,12,32,128]{3,2,1,0:T(8,128)(2,1)S(1)}, u32[]{:S(2)}, u32[]{:S(2)}) collective-permute-start(bf16[5,12,32,128]{3,2,1,0:T(8,128)(2,1)S(1)} %bitcast.144), channel_id=1, source_target_pairs={{2,0},{4,2},{6,4},{8,6},{10,8},{12,10},{14,12},{16,14},{18,16},{20... | collective-permute-start | bytes 1474568 | tf_op jit(solution)/shard_map/ppermute | solution.py:11
  21.3 0.1 slice_bitcast_fusion
  21.5 0.0 copy-start.2
  21.5 0.3 copy.33
  21.9 0.3 copy-done.2
  22.2 20.6 %multiply_convert_fusion.1 = (bf16[1,12,128,768]{3,2,1,0:T(8,128)(2,1)S(1)}, bf16[1,12,128,768]{3,2,1,0:T(8,128)(2,1)S(1)}) fusion(s32[768]{0:T(1024)S(1)} %copy-done.2, s32[12,128]{1,0:T(8,128)S(1)} %multiply_add_fusion), kind=kLoop, calls=%fused_computation.13 | loop fusion | flops 15335424 | bytes 4727808 | tf_op jit(solution)/shard_map/convert.3
  42.8 1.7 fusion.16
  44.5 0.6 copy.17
  45.1 0.4 broadcast_in_dim_reshape.3
  45.5 1.3 copy.18
  46.8 0.0 all-gather.2.cloned.1.call-update
  46.8 11.0 %all-gather.2.cloned.1.call-done = bf16[2,768,640]{2,1,0:T(8,128)(2,1)} async-done(((bf16[1,768,640]{2,1,0:T(8,128)(2,1)}), bf16[2,768,640]{2,1,0:T(8,128)(2,1)}) %all-gather.2.cloned.1.call-update) | async-done | bytes 1966096 | tf_op jit(solution)/shard_map/all_gather | solution.py:56
  57.9 1.6 fusion.41
  59.4 1.6 fusion.40
  61.0 1.6 fusion.39
  62.6 1.6 fusion.38
  64.1 1.6 fusion.37
  65.7 1.6 fusion.36
  67.2 1.6 fusion.35
  68.8 1.6 fusion.34
  70.4 1.6 fusion.33
  71.9 1.6 fusion.32
  73.5 1.6 fusion.31
  75.0 1.6 fusion.30
  76.6 1.6 fusion.29
  78.2 1.6 fusion.28
  79.7 1.6 fusion.27
  81.3 1.6 fusion.26
  82.8 7.0 %all-to-all-start = ((bf16[16,2,48,640]{3,2,1,0:T(8,128)(2,1)}), bf16[16,2,48,640]{3,2,1,0:T(8,128)(2,1)S(1)}, u32[]{:S(2)}, u32[]{:S(2)}) async-start(bf16[16,2,48,640]{3,2,1,0:T(8,128)(2,1)} %fusion.26), calls=%async_computation | async-start | bytes 3932160 | tf_op jit(solution)/shard_map/all_to_all | solution.py:58
  89.8 7.4 %copy.20 = bf16[48,160,384]{2,0,1:T(8,128)(2,1)} copy(bf16[48,160,384]{2,1,0:T(8,128)(2,1)} %param.9) | data formatting | bytes 11796480 | tf_op args[4]
  97.2 0.1 dynamic_slice.3
  97.3 0.1 broadcast_compare_fusion
  97.4 38.1 %all-to-all-done = bf16[16,2,48,640]{3,2,1,0:T(8,128)(2,1)S(1)} async-done(((bf16[16,2,48,640]{3,2,1,0:T(8,128)(2,1)}), bf16[16,2,48,640]{3,2,1,0:T(8,128)(2,1)S(1)}, u32[]{:S(2)}, u32[]{:S(2)}) %all-to-all-start) | async-done | bytes 1966112 | tf_op jit(solution)/shard_map/all_to_all | solution.py:58
  135.5 5.3 %copy.19 = bf16[16,2,48,640]{2,0,3,1:T(8,128)(2,1)} copy(bf16[16,2,48,640]{3,2,1,0:T(8,128)(2,1)S(1)} %all-to-all-done) | data formatting | bytes 3932160 | tf_op jit(solution)/shard_map/all_to_all | solution.py:58
  140.8 15.3 %copy.21 = bf16[2,48,16,2,32,10]{4,2,5,3,0,1:T(8,128)(2,1)} copy(bf16[2,48,16,2,32,10]{1,2,5,4,3,0:T(8,128)(2,1)} %bitcast.135) | data formatting | bytes 3932160 | tf_op jit(solution)/shard_map/reshape;reshape | solution.py:65
  156.2 12.0 %fusion.11 = bf16[48,2,32,2,384]{4,2,3,1,0:T(8,128)(2,1)} fusion(bf16[2,48,16,2,32,10]{4,2,5,3,0,1:T(8,128)(2,1)} %copy.21, bf16[48,16,10,384,1,1]{3,0,2,1,5,4:T(8,128)(2,1)} %bitcast.134), kind=kOutput, calls=%fused_computation.18 | convolution fusion | flops 754974720 | bytes 12582912 | tf_op jit(solution)/shard_map/gsbcvl,sbln->sgvcn/dot_general | solution.py:67
  168.2 3.2 %copy.23 = bf16[48,2,32,2,384]{4,2,1,3,0:T(8,128)(2,1)S(1)} copy(bf16[48,2,32,2,384]{4,2,3,1,0:T(8,128)(2,1)} %fusion.11) | data formatting | bytes 9437184 | tf_op jit(solution)/shard_map/gsbcvl,sbln->sgvcn/transpose | solution.py:67
  171.4 4.2 %fusion = bf16[48,64,2,384]{3,1,2,0:T(8,128)(2,1)} fusion(bf16[48,2,32,2,384]{4,2,1,3,0:T(8,128)(2,1)S(1)} %copy.23, pred[48,384]{1,0:T(8,128)(4,1)S(1)} %broadcast_compare_fusion), kind=kLoop, calls=%fused_computation.1 | loop fusion | flops 2359296 | bytes 9455616 | tf_op jit(solution)/shard_map/convert_element_type | solution.py:74
  175.7 9.5 %copy.24 = bf16[48,64,2,384]{3,2,1,0:T(2,128)(2,1)} copy(bf16[48,64,2,384]{3,1,2,0:T(8,128)(2,1)} %fusion) | data formatting | bytes 9437184 | tf_op jit(solution)/shard_map/convert_element_type | solution.py:74
  (10 shorter events, 0.1 us)
Async XLA Ops:
  6.5 1.2 copy-start
  6.5 51.3 %all-gather.2.cloned.1.call-start = ((), (), s32[]{:S(2)}) async-start(), calls=%async_computation.1 | async-start | bytes 2949120 | tf_op jit(solution)/shard_map/all_gather | solution.py:56
  14.4 28.3 %collective-permute-start = (bf16[5,12,32,128]{3,2,1,0:T(8,128)(2,1)S(1)}, bf16[5,12,32,128]{3,2,1,0:T(8,128)(2,1)S(1)}, u32[]{:S(2)}, u32[]{:S(2)}) collective-permute-start(bf16[5,12,32,128]{3,2,1,0:T(8,128)(2,1)S(1)} %bitcast.143), channel_id=1, source_target_pairs={{0,2},{2,4},{4,6},{6,8},{8,10},{10,12},{12,14},{14,16},{16,18},{18... | collective-permute-start | bytes 1474568 | tf_op jit(solution)/shard_map/ppermute | solution.py:11
  18.0 24.8 %collective-permute-start.1 = (bf16[5,12,32,128]{3,2,1,0:T(8,128)(2,1)S(1)}, bf16[5,12,32,128]{3,2,1,0:T(8,128)(2,1)S(1)}, u32[]{:S(2)}, u32[]{:S(2)}) collective-permute-start(bf16[5,12,32,128]{3,2,1,0:T(8,128)(2,1)S(1)} %bitcast.144), channel_id=1, source_target_pairs={{2,0},{4,2},{6,4},{8,6},{10,8},{12,10},{14,12},{16,14},{18,16},{20... | collective-permute-start | bytes 1474568 | tf_op jit(solution)/shard_map/ppermute | solution.py:11
  21.5 0.7 copy-start.2
  82.8 52.7 %all-to-all-start = ((bf16[16,2,48,640]{3,2,1,0:T(8,128)(2,1)}), bf16[16,2,48,640]{3,2,1,0:T(8,128)(2,1)S(1)}, u32[]{:S(2)}, u32[]{:S(2)}) async-start(bf16[16,2,48,640]{3,2,1,0:T(8,128)(2,1)} %fusion.26), calls=%async_computation | async-start | bytes 3932160 | tf_op jit(solution)/shard_map/all_to_all | solution.py:58
  175.7 9.5 %copy-start.1 = (bf16[10,32,1536]{2,1,0:T(8,128)(2,1)S(1)}, bf16[10,32,1536]{2,1,0:T(8,128)(2,1)}, u32[]{:S(2)}) copy-start(bf16[10,32,1536]{2,1,0:T(8,128)(2,1)} %param.5) | copy-start | bytes 2949124
Sparse Core Ops, SparseCore 0:
  46.9 10.8 all-gather.1
